TPU v7x, 512 devices: a whole 4x4x16 slice. The times are simulated.
512 devices in a mesh: obj: 16 (over x, z_hi, core), tile: 32 (over y, z_lo).
Axes of the slice: x: 4, y: 4, z: 16 (z_hi: 2, z_lo: 8; z = z_hi * 8 + z_lo), core: 2. Of those that a mesh axis runs over, the one named last changes fastest.
Arguments:
- checkpoints: bfloat16 [6, 12, 48, 32, 128], P(None, None, 'obj', 'tile'), may hold values from 0.19921875 to 2
- courant: float32 [2, 48, 32, 128], P(None, None, 'tile'), may hold values from -0.6 to 0.6
- insolation: float32 [32, 128], P('tile'), may hold values from 0.3 to 3
- region_mask: int32 [16, 32, 128], P('obj', 'tile'), may hold values 0 or 1
- measure_step: int32 [16], P('obj'), may hold values from 1 to 6
- snr_weight: float32 [12, 48], replicated, may hold values from 0.3 to 3
- diffusion_number: float32 [12, 47], replicated, may hold values from 0.1 to 2
- coupling: float32 [12, 12], replicated, may hold values from -1.75 to 1.75
- recombination: float32 [12], replicated, may hold values from 0.05 to 0.25
Outputs:
- state_adjoint: float32 [16, 12, 48, 32, 128], P('obj', None, None, 'tile')
- driver_grad: float32 [16, 6, 12, 48], P('obj')
All inputs are finite; a program needn't handle non-finite values. No bound on the sum of `region_mask` on one device may be relied on, other than what follows from the above.
Results may differ from a plain program's by a relative error of at most 0.0003.
Values may be sent and summed in bfloat16 or wider, within the bound.
A program may use at most 64 MiB of HBM per device.

v0:
```python
import jax
import jax.numpy as jnp
from jax import lax
from jax.sharding import PartitionSpec as P

smoothing = 0.2


def padded_2(block, sides, width):
    for axis, dim in sides:
        count = lax.axis_size(axis)
        forward = [(i, i + 1) for i in range(count - 1)]
        forward.append((count - 1, 0))
        backward = [(target, source) for source, target in forward]
        low = lax.ppermute(
            lax.slice_in_dim(block, block.shape[dim] - width, None, axis=dim), axis, forward
        )
        high = lax.ppermute(lax.slice_in_dim(block, 0, width, axis=dim), axis, backward)
        block = jnp.concatenate([low, block, high], axis=dim)
    return block


def advect_back(adjoint, padded, flux, northward):
    lat_pad = jnp.pad(adjoint, ((0, 0), (0, 0), (0, 0), (1, 1)))
    north_flux = jnp.pad(northward[None] * adjoint, ((0, 0), (0, 0), (0, 0), (1, 1)))
    beside_all = padded[:, :, 2:] + padded[:, :, :-2] + lat_pad[..., 2:] + lat_pad[..., :-2]
    carried = flux[:, :, 2:] - flux[:, :, :-2] + north_flux[..., 2:] - north_flux[..., :-2]
    return (1.0 - 4.0 * smoothing) * adjoint + smoothing * beside_all + 0.5 * carried


def react_back(solved, state, coupling, recombination):
    mixing = jnp.einsum("fg,...flxy->...glxy", coupling, solved, precision=lax.Precision.HIGHEST)
    return (
        solved
        + mixing
        - 2.0 * recombination[:, None, None, None] * state.astype(jnp.float32) * solved
    )


def per_device(
    checkpoints,
    courant,
    insolation,
    region_mask,
    measure_step,
    snr_weight,
    diffusion_number,
    coupling,
    recombination,
):
    steps = checkpoints.shape[0]
    fields, levels = snr_weight.shape
    width, latitudes = insolation.shape
    columns = width * latitudes
    cells = columns * lax.axis_size("tile")
    impulse = region_mask[0].astype(jnp.float32)[None, None] * snr_weight[:, :, None, None]
    below = jnp.pad(diffusion_number, ((0, 0), (1, 0)))
    above = jnp.pad(diffusion_number, ((0, 0), (0, 1)))
    middle = 1.0 + below + above
    eastward = courant[0]
    northward = courant[1]
    adjoint = jnp.zeros((fields, levels, width, latitudes), jnp.float32)
    partials = [None] * steps
    for back in range(steps):
        moment = steps - 1 - back
        arrive = (measure_step[0] == moment + 1).astype(jnp.float32)
        adjoint = adjoint + arrive * impulse
        stacked = jnp.stack([adjoint, eastward[None] * adjoint])
        extended = padded_2(stacked, (("tile", 3),), 1)
        padded = extended[0]
        flux = extended[1]
        advected = advect_back(adjoint, padded, flux, northward)
        solved = lax.linalg.tridiagonal_solve(
            -below, middle, -above, advected.reshape(fields, levels, columns)
        )
        solved = solved.reshape(fields, levels, width, latitudes)
        partial_sum = jnp.einsum("flxy,xy->fl", solved, insolation, precision=lax.Precision.HIGHEST)
        partial_sum = lax.psum(partial_sum, "tile")
        partials[moment] = partial_sum
        state = checkpoints[moment]
        adjoint = react_back(
            solved, lax.all_gather(state, "obj", axis=1, tiled=True), coupling, recombination
        )
    gradients = jnp.stack(partials)
    return (adjoint[None], (gradients / cells)[None])


def solution(mesh):
    return jax.shard_map(
        per_device,
        mesh=mesh,
        in_specs=(
            P(None, None, "obj", "tile", None),
            P(None, None, "tile", None),
            P("tile", None),
            P("obj", "tile", None),
            P("obj"),
            P(),
            P(),
            P(),
            P(),
        ),
        out_specs=(P("obj", None, None, "tile", None), P("obj", None, None, None)),
        check_vma=False,
    )
```

profile of v0, /device:TPU:2, one launch (start us, length us, event | category | flops | bytes accessed | tf_op | source)
XLA Modules:
  0.0 679.5 jit_solution(14576754906486607328)
XLA Ops:
  4.0 15.6 %collective-permute-start.1 = (f32[2,12,48,1,128]{4,2,3,1,0:T(8,128)S(1)}, f32[2,12,48,1,128]{4,2,3,1,0:T(8,128)S(1)}, u32[]{:S(2)}, u32[]{:S(2)}) collective-permute-start(f32[2,12,48,1,128]{4,2,3,1,0:T(8,128)S(1)} %copy.30), channel_id=1, source_target_pairs={{1,0},{2,1},{3,2},{4,3},{5,4},{6,5},{7,6},{8,7},{9,8},{10,9},{11,1... | collective-permute-start | bytes 1769480 | tf_op jit(solution)/shard_map/ppermute | solution.py:18
  19.6 1.9 collective-permute-start
  22.8 53.9 %all-gather = bf16[1,12,48,1,128]{4,1,3,0,2:T(8,128)(2,1)S(1)} all-gather(bf16[1,12,3,1,128]{4,1,3,0,2:T(8,128)(2,1)S(1)} %copy.99), channel_id=2, replica_groups=mesh['obj'=16,'tile'=32] {'obj'}, dimensions={2}, use_global_device_ids=true | all-gather | bytes 156672 | tf_op jit(solution)/shard_map/all_gather | solution.py:82
  82.4 3.4 collective-permute-start.3
  85.8 2.5 collective-permute-start.2
  88.3 57.2 %all-gather.1 = bf16[1,12,48,1,128]{4,1,3,0,2:T(8,128)(2,1)S(1)} all-gather(bf16[1,12,3,1,128]{4,1,3,0,2:T(8,128)(2,1)S(1)} %copy.100), channel_id=3, replica_groups=mesh['obj'=16,'tile'=32] {'obj'}, dimensions={2}, use_global_device_ids=true | all-gather | bytes 156672 | tf_op jit(solution)/shard_map/all_gather | solution.py:82
  151.0 4.8 collective-permute-start.5
  155.8 1.9 collective-permute-start.4
  157.7 57.7 %all-gather.2 = bf16[1,12,48,1,128]{4,1,3,0,2:T(8,128)(2,1)S(1)} all-gather(bf16[1,12,3,1,128]{4,1,3,0,2:T(8,128)(2,1)S(1)} %copy.101), channel_id=4, replica_groups=mesh['obj'=16,'tile'=32] {'obj'}, dimensions={2}, use_global_device_ids=true | all-gather | bytes 156672 | tf_op jit(solution)/shard_map/all_gather | solution.py:82
  221.0 5.3 collective-permute-start.7
  226.3 1.9 collective-permute-start.6
  228.3 58.2 %all-gather.5 = bf16[1,12,48,1,128]{4,1,3,0,2:T(8,128)(2,1)S(1)} all-gather(bf16[1,12,3,1,128]{4,1,3,0,2:T(8,128)(2,1)S(1)} %copy.104), channel_id=7, replica_groups=mesh['obj'=16,'tile'=32] {'obj'}, dimensions={2}, use_global_device_ids=true | all-gather | bytes 156672 | tf_op jit(solution)/shard_map/all_gather | solution.py:82
  286.5 34.6 %all-gather.3 = bf16[1,12,48,1,128]{4,1,3,0,2:T(8,128)(2,1)S(1)} all-gather(bf16[1,12,3,1,128]{4,1,3,0,2:T(8,128)(2,1)S(1)} %copy.102), channel_id=5, replica_groups=mesh['obj'=16,'tile'=32] {'obj'}, dimensions={2}, use_global_device_ids=true | all-gather | bytes 156672 | tf_op jit(solution)/shard_map/all_gather | solution.py:82
  321.0 45.1 %all-gather.4 = bf16[1,12,48,1,128]{4,1,3,0,2:T(8,128)(2,1)S(1)} all-gather(bf16[1,12,3,1,128]{4,1,3,0,2:T(8,128)(2,1)S(1)} %copy.103), channel_id=6, replica_groups=mesh['obj'=16,'tile'=32] {'obj'}, dimensions={2}, use_global_device_ids=true | all-gather | bytes 156672 | tf_op jit(solution)/shard_map/all_gather | solution.py:82
  372.7 7.7 %collective-permute-start.9 = (f32[2,12,48,1,128]{4,2,3,1,0:T(8,128)S(1)}, f32[2,12,48,1,128]{4,2,3,1,0:T(8,128)S(1)}, u32[]{:S(2)}, u32[]{:S(2)}) collective-permute-start(f32[2,12,48,1,128]{4,2,3,1,0:T(8,128)S(1)} %copy.60), channel_id=1, source_target_pairs={{1,0},{2,1},{3,2},{4,3},{5,4},{6,5},{7,6},{8,7},{9,8},{10,9},{11,1... | collective-permute-start | bytes 1769480 | tf_op jit(solution)/shard_map/ppermute | solution.py:18
  380.4 2.1 collective-permute-start.8
  384.6 9.5 %collective-permute-done.9 = f32[2,12,48,1,128]{4,2,3,1,0:T(8,128)S(1)} collective-permute-done((f32[2,12,48,1,128]{4,2,3,1,0:T(8,128)S(1)}, f32[2,12,48,1,128]{4,2,3,1,0:T(8,128)S(1)}, u32[]{:S(2)}, u32[]{:S(2)}) %collective-permute-start.9) | collective-permute-done | bytes 589856 | tf_op jit(solution)/shard_map/ppermute | solution.py:18
  394.3 12.6 %collective-permute-done.8 = f32[2,12,48,1,128]{4,2,3,1,0:T(8,128)S(1)} collective-permute-done((f32[2,12,48,1,128]{4,2,3,1,0:T(8,128)S(1)}, f32[2,12,48,1,128]{4,2,3,1,0:T(8,128)S(1)}, u32[]{:S(2)}, u32[]{:S(2)}) %collective-permute-start.8) | collective-permute-done | bytes 589856 | tf_op jit(solution)/shard_map/ppermute | solution.py:15
  412.2 5.6 collective-permute-start.11
  417.8 1.9 collective-permute-start.10
  421.7 19.9 %collective-permute-done.11 = f32[2,12,48,1,128]{4,2,3,1,0:T(8,128)S(1)} collective-permute-done((f32[2,12,48,1,128]{4,2,3,1,0:T(8,128)S(1)}, f32[2,12,48,1,128]{4,2,3,1,0:T(8,128)S(1)}, u32[]{:S(2)}, u32[]{:S(2)}) %collective-permute-start.11) | collective-permute-done | bytes 589856 | tf_op jit(solution)/shard_map/ppermute | solution.py:18
  441.9 1.7 collective-permute-done.10
  448.5 1.0 copy.74
  450.5 228.3 %all-reduce.14 = (f32[1,1,12,48]{3,0,2,1:T(1,128)S(1)}, f32[1,1,12,48]{3,0,2,1:T(1,128)S(1)}, f32[1,1,12,48]{3,0,2,1:T(1,128)S(1)}, f32[1,1,12,48]{3,0,2,1:T(1,1...) all-reduce(f32[1,1,12,48]{3,0,2,1:T(1,128)S(1)} %stack.87, ...), channel_id=1, replica_groups=mesh['obj'=16,'tile'=32] {'tile'}, use_global_device_ids=true, to_apply=%region_0.1 | all-reduce | flops 3456 | bytes 27648 | tf_op jit(solution)/shard_map/psum | solution.py:78
  (422 shorter events, 42.9 us)
Async XLA Ops:
  0.6 80.8 %copy-start = (f32[12,12]{1,0:T(8,128)S(1)}, f32[12,12]{1,0:T(8,128)}, u32[]{:S(2)}) copy-start(f32[12,12]{1,0:T(8,128)} %param.16) | copy-start | bytes 1732
  0.6 20.9 %copy-start.3 = (f32[12,47]{1,0:T(8,128)S(1)}, f32[12,47]{1,0:T(8,128)}, u32[]{:S(2)}) copy-start(f32[12,47]{1,0:T(8,128)} %param.15) | copy-start | bytes 6772
  0.7 21.1 %copy-start.1 = (bf16[6,12,3,1,128]{4,2,3,1,0:T(4,128)(2,1)S(1)}, bf16[6,12,3,1,128]{4,2,3,1,0:T(4,128)(2,1)}, u32[]{:S(2)}) copy-start(bf16[6,12,3,1,128]{4,2,3,1,0:T(4,128)(2,1)} %param.9) | copy-start | bytes 165892
  0.7 22.1 %copy-start.4 = (f32[12]{0:T(128)S(1)}, f32[12]{0:T(128)}, u32[]{:S(2)}) copy-start(f32[12]{0:T(128)} %param.17) | copy-start | bytes 148
  4.0 72.9 %collective-permute-start.1 = (f32[2,12,48,1,128]{4,2,3,1,0:T(8,128)S(1)}, f32[2,12,48,1,128]{4,2,3,1,0:T(8,128)S(1)}, u32[]{:S(2)}, u32[]{:S(2)}) collective-permute-start(f32[2,12,48,1,128]{4,2,3,1,0:T(8,128)S(1)} %copy.30), channel_id=1, source_target_pairs={{1,0},{2,1},{3,2},{4,3},{5,4},{6,5},{7,6},{8,7},{9,8},{10,9},{11,1... | collective-permute-start | bytes 1769480 | tf_op jit(solution)/shard_map/ppermute | solution.py:18
  19.6 57.5 %collective-permute-start = (f32[2,12,48,1,128]{4,2,3,1,0:T(8,128)S(1)}, f32[2,12,48,1,128]{4,2,3,1,0:T(8,128)S(1)}, u32[]{:S(2)}, u32[]{:S(2)}) collective-permute-start(f32[2,12,48,1,128]{4,2,3,1,0:T(8,128)S(1)} %copy.30), channel_id=1, source_target_pairs={{0,1},{1,2},{2,3},{3,4},{4,5},{5,6},{6,7},{7,8},{8,9},{9,10},{10,1... | collective-permute-start | bytes 1769480 | tf_op jit(solution)/shard_map/ppermute | solution.py:15
  82.4 63.0 %collective-permute-start.3 = (f32[2,12,48,1,128]{4,2,3,1,0:T(8,128)S(1)}, f32[2,12,48,1,128]{4,2,3,1,0:T(8,128)S(1)}, u32[]{:S(2)}, u32[]{:S(2)}) collective-permute-start(f32[2,12,48,1,128]{4,2,3,1,0:T(8,128)S(1)} %copy.39), channel_id=1, source_target_pairs={{1,0},{2,1},{3,2},{4,3},{5,4},{6,5},{7,6},{8,7},{9,8},{10,9},{11,1... | collective-permute-start | bytes 1769480 | tf_op jit(solution)/shard_map/ppermute | solution.py:18
  85.8 59.8 %collective-permute-start.2 = (f32[2,12,48,1,128]{4,2,3,1,0:T(8,128)S(1)}, f32[2,12,48,1,128]{4,2,3,1,0:T(8,128)S(1)}, u32[]{:S(2)}, u32[]{:S(2)}) collective-permute-start(f32[2,12,48,1,128]{4,2,3,1,0:T(8,128)S(1)} %copy.39), channel_id=1, source_target_pairs={{0,1},{1,2},{2,3},{3,4},{4,5},{5,6},{6,7},{7,8},{8,9},{9,10},{10,1... | collective-permute-start | bytes 1769480 | tf_op jit(solution)/shard_map/ppermute | solution.py:15
  151.0 64.5 %collective-permute-start.5 = (f32[2,12,48,1,128]{4,2,3,1,0:T(8,128)S(1)}, f32[2,12,48,1,128]{4,2,3,1,0:T(8,128)S(1)}, u32[]{:S(2)}, u32[]{:S(2)}) collective-permute-start(f32[2,12,48,1,128]{4,2,3,1,0:T(8,128)S(1)} %copy.46), channel_id=1, source_target_pairs={{1,0},{2,1},{3,2},{4,3},{5,4},{6,5},{7,6},{8,7},{9,8},{10,9},{11,1... | collective-permute-start | bytes 1769480 | tf_op jit(solution)/shard_map/ppermute | solution.py:18
  155.8 59.9 %collective-permute-start.4 = (f32[2,12,48,1,128]{4,2,3,1,0:T(8,128)S(1)}, f32[2,12,48,1,128]{4,2,3,1,0:T(8,128)S(1)}, u32[]{:S(2)}, u32[]{:S(2)}) collective-permute-start(f32[2,12,48,1,128]{4,2,3,1,0:T(8,128)S(1)} %copy.46), channel_id=1, source_target_pairs={{0,1},{1,2},{2,3},{3,4},{4,5},{5,6},{6,7},{7,8},{8,9},{9,10},{10,1... | collective-permute-start | bytes 1769480 | tf_op jit(solution)/shard_map/ppermute | solution.py:15
  220.8 145.4 %copy-start.2 = (f32[1,128]{1,0:T(1,128)S(1)}, f32[1,128]{1,0:T(1,128)}, u32[]{:S(2)}) copy-start(f32[1,128]{1,0:T(1,128)} %param.11) | copy-start | bytes 1540
  221.0 146.1 %collective-permute-start.7 = (f32[2,12,48,1,128]{4,2,3,1,0:T(8,128)S(1)}, f32[2,12,48,1,128]{4,2,3,1,0:T(8,128)S(1)}, u32[]{:S(2)}, u32[]{:S(2)}) collective-permute-start(f32[2,12,48,1,128]{4,2,3,1,0:T(8,128)S(1)} %copy.53), channel_id=1, source_target_pairs={{1,0},{2,1},{3,2},{4,3},{5,4},{6,5},{7,6},{8,7},{9,8},{10,9},{11,1... | collective-permute-start | bytes 1769480 | tf_op jit(solution)/shard_map/ppermute | solution.py:18
  226.3 141.0 %collective-permute-start.6 = (f32[2,12,48,1,128]{4,2,3,1,0:T(8,128)S(1)}, f32[2,12,48,1,128]{4,2,3,1,0:T(8,128)S(1)}, u32[]{:S(2)}, u32[]{:S(2)}) collective-permute-start(f32[2,12,48,1,128]{4,2,3,1,0:T(8,128)S(1)} %copy.53), channel_id=1, source_target_pairs={{0,1},{1,2},{2,3},{3,4},{4,5},{5,6},{6,7},{7,8},{8,9},{9,10},{10,1... | collective-permute-start | bytes 1769480 | tf_op jit(solution)/shard_map/ppermute | solution.py:15
  372.7 21.4 %collective-permute-start.9 = (f32[2,12,48,1,128]{4,2,3,1,0:T(8,128)S(1)}, f32[2,12,48,1,128]{4,2,3,1,0:T(8,128)S(1)}, u32[]{:S(2)}, u32[]{:S(2)}) collective-permute-start(f32[2,12,48,1,128]{4,2,3,1,0:T(8,128)S(1)} %copy.60), channel_id=1, source_target_pairs={{1,0},{2,1},{3,2},{4,3},{5,4},{6,5},{7,6},{8,7},{9,8},{10,9},{11,1... | collective-permute-start | bytes 1769480 | tf_op jit(solution)/shard_map/ppermute | solution.py:18
  380.4 26.5 %collective-permute-start.8 = (f32[2,12,48,1,128]{4,2,3,1,0:T(8,128)S(1)}, f32[2,12,48,1,128]{4,2,3,1,0:T(8,128)S(1)}, u32[]{:S(2)}, u32[]{:S(2)}) collective-permute-start(f32[2,12,48,1,128]{4,2,3,1,0:T(8,128)S(1)} %copy.60), channel_id=1, source_target_pairs={{0,1},{1,2},{2,3},{3,4},{4,5},{5,6},{6,7},{7,8},{8,9},{9,10},{10,1... | collective-permute-start | bytes 1769480 | tf_op jit(solution)/shard_map/ppermute | solution.py:15
  412.2 29.5 %collective-permute-start.11 = (f32[2,12,48,1,128]{4,2,3,1,0:T(8,128)S(1)}, f32[2,12,48,1,128]{4,2,3,1,0:T(8,128)S(1)}, u32[]{:S(2)}, u32[]{:S(2)}) collective-permute-start(f32[2,12,48,1,128]{4,2,3,1,0:T(8,128)S(1)} %copy.67), channel_id=1, source_target_pairs={{1,0},{2,1},{3,2},{4,3},{5,4},{6,5},{7,6},{8,7},{9,8},{10,9},{11,1... | collective-permute-start | bytes 1769480 | tf_op jit(solution)/shard_map/ppermute | solution.py:18
  417.8 25.8 %collective-permute-start.10 = (f32[2,12,48,1,128]{4,2,3,1,0:T(8,128)S(1)}, f32[2,12,48,1,128]{4,2,3,1,0:T(8,128)S(1)}, u32[]{:S(2)}, u32[]{:S(2)}) collective-permute-start(f32[2,12,48,1,128]{4,2,3,1,0:T(8,128)S(1)} %copy.67), channel_id=1, source_target_pairs={{0,1},{1,2},{2,3},{3,4},{4,5},{5,6},{6,7},{7,8},{8,9},{9,10},{10,1... | collective-permute-start | bytes 1769480 | tf_op jit(solution)/shard_map/ppermute | solution.py:15
where the time goes:
time: 680 us
  blocking collectives  535 us (79%)
  starting transfers between devices  54.6 us (8%)
  waiting for transfers between devices  43.7 us (6%)
  other arithmetic  26.3 us (4%)
  matrix products  9.1 us (1%)
  local copies, waits for them, and re-layouts  8.41 us (1%)
    all_gather x6, blocking collectives, per_device(): lax.all_gather(state, 'obj', axis=1, tiled=True)  307 us
    psum x1, blocking collectives, per_device(): partial_sum = lax.psum(partial_sum, 'tile')  228 us
    ppermute x6, starting transfers between devices, padded_2(): lax.ppermute(lax.slice_in_dim(block, 0, width, axis=dim), axis, backward)  42.3 us
    ppermute x6, waiting for transfers between devices, padded_2(): lax.ppermute(lax.slice_in_dim(block, 0, width, axis=dim), axis, backward)  29.4 us
    unnamed x144, other arithmetic  14.8 us
    ppermute x6, waiting for transfers between devices, padded_2(): lax.ppermute(lax.slice_in_dim(block, block.shape[dim] - width, None, axis...  14.3 us
  transfers between devices with their start and end apart: 12, of which 4 were waited for; matrix products, arithmetic and copies ran while one was open for 1% of the time, Pallas kernels for 0%

commit v1 on v0

--- a/solution.py
+++ b/solution.py
@@ -75,7 +75,7 @@
         )
         solved = solved.reshape(fields, levels, width, latitudes)
         partial_sum = jnp.einsum("flxy,xy->fl", solved, insolation, precision=lax.Precision.HIGHEST)
-        partial_sum = lax.psum(partial_sum, "tile")
+        partial_sum = jnp.sum(lax.all_gather(partial_sum, "tile"), axis=0)
         partials[moment] = partial_sum
         state = checkpoints[moment]
         adjoint = react_back(

time: 680 us -> 1320 us (1.94)
  blocking collectives: 535 us -> 1010 us
  other arithmetic: 26.3 us -> 181 us
  waiting for transfers between devices: 43.7 us -> 0.03 us
  local copies, waits for them, and re-layouts: 8.41 us -> 50.1 us
    all_gather x0 -> x6, blocking collectives: none -> 705 us  [per_device(): partial_sum = jnp.sum(lax.all_gather(partial_sum, 'tile'), axis=0)]
    psum x1 -> x0, blocking collectives: 228 us -> none  [per_device(): partial_sum = lax.psum(partial_sum, 'tile')]
    unnamed x144, other arithmetic: 14.8 us -> 146 us
    unnamed x156 -> x468, local copies, waits for them, and re-layouts: 2.21 us -> 42.1 us
    ppermute x6, waiting for transfers between devices: 29.4 us -> 0.02 us  [padded_2(): lax.ppermute(lax.slice_in_dim(block, 0, width, axis=dim), axis, backward)]
    ppermute x6, waiting for transfers between devices: 14.3 us -> 0.02 us  [padded_2(): lax.ppermute(lax.slice_in_dim(block, block.shape[dim] - width, None, axis...]
  transfers between devices with their start and end apart: 12 -> 12, of which waited for: 4 -> 0; matrix products, arithmetic and copies ran while one was open for 1% -> 2% of each run, Pallas kernels for 0% -> 0%
where the time goes in v1:
time: 1320 us; the launch traced here: 1310 us
  blocking collectives  1010 us (77%)
  other arithmetic  181 us (14%)
  local copies, waits for them, and re-layouts  50.1 us (4%)
  starting transfers between devices  47.5 us (4%)
  matrix products  15.9 us (1%)
    all_gather x6, blocking collectives, per_device(): partial_sum = jnp.sum(lax.all_gather(partial_sum, 'tile'), axis=0)  705 us
    all_gather x6, blocking collectives, per_device(): lax.all_gather(state, 'obj', axis=1, tiled=True)  304 us
    unnamed x144, other arithmetic  146 us
    unnamed x468, local copies, waits for them, and re-layouts  42.1 us
    ppermute x6, starting transfers between devices, padded_2(): lax.ppermute(lax.slice_in_dim(block, 0, width, axis=dim), axis, backward)  35.1 us
  transfers between devices with their start and end apart: 12, of which 0 were waited for; matrix products, arithmetic and copies ran while one was open for 2% of the time, Pallas kernels for 0%

profile of v1, /device:TPU:2, one launch (start us, length us, event | category | flops | bytes accessed | tf_op | source)
XLA Modules:
  0.0 1308.0 jit_solution(6375031107303281486)
XLA Ops:
  5.2 15.6 %collective-permute-start.1 = (f32[2,12,48,1,128]{4,2,3,1,0:T(8,128)S(1)}, f32[2,12,48,1,128]{4,2,3,1,0:T(8,128)S(1)}, u32[]{:S(2)}, u32[]{:S(2)}) collective-permute-start(f32[2,12,48,1,128]{4,2,3,1,0:T(8,128)S(1)} %copy.30), channel_id=1, source_target_pairs={{1,0},{2,1},{3,2},{4,3},{5,4},{6,5},{7,6},{8,7},{9,8},{10,9},{11,1... | collective-permute-start | bytes 1769480 | tf_op jit(solution)/shard_map/ppermute | solution.py:18
  29.2 48.8 %all-gather = bf16[1,12,48,1,128]{4,1,3,0,2:T(8,128)(2,1)S(1)} all-gather(bf16[1,12,3,1,128]{4,1,3,0,2:T(8,128)(2,1)S(1)} %copy.99), channel_id=2, replica_groups=mesh['obj'=16,'tile'=32] {'obj'}, dimensions={2}, use_global_device_ids=true | all-gather | bytes 156672 | tf_op jit(solution)/shard_map/all_gather | solution.py:82
  101.1 4.3 collective-permute-start.3
  107.4 57.5 %all-gather.1 = bf16[1,12,48,1,128]{4,1,3,0,2:T(8,128)(2,1)S(1)} all-gather(bf16[1,12,3,1,128]{4,1,3,0,2:T(8,128)(2,1)S(1)} %copy.100), channel_id=3, replica_groups=mesh['obj'=16,'tile'=32] {'obj'}, dimensions={2}, use_global_device_ids=true | all-gather | bytes 156672 | tf_op jit(solution)/shard_map/all_gather | solution.py:82
  166.4 2.6 fusion.959
  188.1 4.0 collective-permute-start.5
  194.1 57.7 %all-gather.5 = bf16[1,12,48,1,128]{4,1,3,0,2:T(8,128)(2,1)S(1)} all-gather(bf16[1,12,3,1,128]{4,1,3,0,2:T(8,128)(2,1)S(1)} %copy.104), channel_id=7, replica_groups=mesh['obj'=16,'tile'=32] {'obj'}, dimensions={2}, use_global_device_ids=true | all-gather | bytes 156672 | tf_op jit(solution)/shard_map/all_gather | solution.py:82
  251.8 36.6 %all-gather.2 = bf16[1,12,48,1,128]{4,1,3,0,2:T(8,128)(2,1)S(1)} all-gather(bf16[1,12,3,1,128]{4,1,3,0,2:T(8,128)(2,1)S(1)} %copy.101), channel_id=4, replica_groups=mesh['obj'=16,'tile'=32] {'obj'}, dimensions={2}, use_global_device_ids=true | all-gather | bytes 156672 | tf_op jit(solution)/shard_map/all_gather | solution.py:82
  291.9 2.2 constant_dynamic-update-slice_fusion.140
  339.7 4.2 collective-permute-start.7
  345.8 58.3 %all-gather.3 = bf16[1,12,48,1,128]{4,1,3,0,2:T(8,128)(2,1)} all-gather(bf16[1,12,3,1,128]{4,1,3,0,2:T(8,128)(2,1)S(1)} %copy.102), channel_id=5, replica_groups=mesh['obj'=16,'tile'=32] {'obj'}, dimensions={2}, use_global_device_ids=true | all-gather | bytes 156672 | tf_op jit(solution)/shard_map/all_gather | solution.py:82
  404.0 45.6 %all-gather.4 = bf16[1,12,48,1,128]{4,1,3,0,2:T(8,128)(2,1)} all-gather(bf16[1,12,3,1,128]{4,1,3,0,2:T(8,128)(2,1)S(1)} %copy.103), channel_id=6, replica_groups=mesh['obj'=16,'tile'=32] {'obj'}, dimensions={2}, use_global_device_ids=true | all-gather | bytes 156672 | tf_op jit(solution)/shard_map/all_gather | solution.py:82
  450.6 114.7 %all-gather.17 = f32[32,12,48]{2,1,0:T(8,128)S(1)} all-gather(f32[1,12,48]{2,1,0:T(8,128)S(1)} %copy.92), channel_id=13, replica_groups=mesh['obj'=16,'tile'=32] {'tile'}, dimensions={0}, use_global_device_ids=true | all-gather | bytes 76032 | tf_op jit(solution)/shard_map/all_gather | solution.py:78
  571.2 2.2 constant_dynamic-update-slice_fusion.187
  618.4 3.2 collective-permute-start.9
  621.7 2.6 collective-permute-start.8
  625.3 123.5 %all-gather.16 = f32[32,12,48]{2,1,0:T(8,128)S(1)} all-gather(f32[1,12,48]{2,1,0:T(8,128)S(1)} %copy.90), channel_id=12, replica_groups=mesh['obj'=16,'tile'=32] {'tile'}, dimensions={0}, use_global_device_ids=true | all-gather | bytes 76032 | tf_op jit(solution)/shard_map/all_gather | solution.py:78
  752.0 113.7 %all-gather.15 = f32[32,12,48]{2,1,0:T(8,128)S(1)} all-gather(f32[1,12,48]{2,1,0:T(8,128)S(1)} %copy.88), channel_id=11, replica_groups=mesh['obj'=16,'tile'=32] {'tile'}, dimensions={0}, use_global_device_ids=true | all-gather | bytes 76032 | tf_op jit(solution)/shard_map/all_gather | solution.py:78
  871.6 2.2 constant_dynamic-update-slice_fusion.234
  918.8 3.7 collective-permute-start.11
  922.6 2.1 collective-permute-start.10
  925.7 124.0 %all-gather.14 = f32[32,12,48]{2,1,0:T(8,128)S(1)} all-gather(f32[1,12,48]{2,1,0:T(8,128)S(1)} %copy.86), channel_id=10, replica_groups=mesh['obj'=16,'tile'=32] {'tile'}, dimensions={0}, use_global_device_ids=true | all-gather | bytes 76032 | tf_op jit(solution)/shard_map/all_gather | solution.py:78
  1052.9 113.6 %all-gather.13 = f32[32,12,48]{2,1,0:T(8,128)S(1)} all-gather(f32[1,12,48]{2,1,0:T(8,128)S(1)} %copy.84), channel_id=9, replica_groups=mesh['obj'=16,'tile'=32] {'tile'}, dimensions={0}, use_global_device_ids=true | all-gather | bytes 76032 | tf_op jit(solution)/shard_map/all_gather | solution.py:78
  1191.7 115.2 %all-gather.12 = f32[32,12,48]{2,1,0:T(8,128)S(1)} all-gather(f32[1,12,48]{2,1,0:T(8,128)S(1)} %copy.82), channel_id=8, replica_groups=mesh['obj'=16,'tile'=32] {'tile'}, dimensions={0}, use_global_device_ids=true | all-gather | bytes 76032 | tf_op jit(solution)/shard_map/all_gather | solution.py:78
  (739 shorter events, 244.9 us)
Async XLA Ops:
  3.4 334.3 %copy-start.2 = (f32[12,48]{0,1:T(8,128)}, f32[12,48]{0,1:T(8,128)S(1)}, u32[]{:S(2)}) copy-start(f32[12,48]{0,1:T(8,128)S(1)} %copy.28) | copy-start | bytes 6916
  5.2 73.6 %collective-permute-start.1 = (f32[2,12,48,1,128]{4,2,3,1,0:T(8,128)S(1)}, f32[2,12,48,1,128]{4,2,3,1,0:T(8,128)S(1)}, u32[]{:S(2)}, u32[]{:S(2)}) collective-permute-start(f32[2,12,48,1,128]{4,2,3,1,0:T(8,128)S(1)} %copy.30), channel_id=1, source_target_pairs={{1,0},{2,1},{3,2},{4,3},{5,4},{6,5},{7,6},{8,7},{9,8},{10,9},{11,1... | collective-permute-start | bytes 1769480 | tf_op jit(solution)/shard_map/ppermute | solution.py:18
  20.8 58.2 %collective-permute-start = (f32[2,12,48,1,128]{4,2,3,1,0:T(8,128)S(1)}, f32[2,12,48,1,128]{4,2,3,1,0:T(8,128)S(1)}, u32[]{:S(2)}, u32[]{:S(2)}) collective-permute-start(f32[2,12,48,1,128]{4,2,3,1,0:T(8,128)S(1)} %copy.30), channel_id=1, source_target_pairs={{0,1},{1,2},{2,3},{3,4},{4,5},{5,6},{6,7},{7,8},{8,9},{9,10},{10,1... | collective-permute-start | bytes 1769480 | tf_op jit(solution)/shard_map/ppermute | solution.py:15
  23.5 309.2 %copy-start.22 = (f32[12]{0:T(128)}, f32[12]{0:T(128)S(1)}, u32[]{:S(2)}) copy-start(f32[12]{0:T(128)S(1)} %get-tuple-element.716) | copy-start | bytes 148
  23.5 309.2 %copy-start.25 = (f32[12]{0:T(128)}, f32[12]{0:T(128)S(1)}, u32[]{:S(2)}) copy-start(f32[12]{0:T(128)S(1)} %get-tuple-element.717) | copy-start | bytes 148
  23.5 309.2 %copy-start.28 = (f32[12]{0:T(128)}, f32[12]{0:T(128)S(1)}, u32[]{:S(2)}) copy-start(f32[12]{0:T(128)S(1)} %get-tuple-element.719) | copy-start | bytes 148
  23.6 309.2 %copy-start.31 = (f32[12]{0:T(128)}, f32[12]{0:T(128)S(1)}, u32[]{:S(2)}) copy-start(f32[12]{0:T(128)S(1)} %get-tuple-element.721) | copy-start | bytes 148
  23.6 309.2 %copy-start.34 = (f32[12]{0:T(128)}, f32[12]{0:T(128)S(1)}, u32[]{:S(2)}) copy-start(f32[12]{0:T(128)S(1)} %get-tuple-element.723) | copy-start | bytes 148
  24.9 307.9 %copy-start.37 = (f32[12]{0:T(128)}, f32[12]{0:T(128)S(1)}, u32[]{:S(2)}) copy-start(f32[12]{0:T(128)S(1)} %get-tuple-element.697) | copy-start | bytes 148
  24.9 307.9 %copy-start.41 = (f32[12]{0:T(128)}, f32[12]{0:T(128)S(1)}, u32[]{:S(2)}) copy-start(f32[12]{0:T(128)S(1)} %get-tuple-element.712) | copy-start | bytes 148
  24.9 307.9 %copy-start.45 = (f32[12]{0:T(128)}, f32[12]{0:T(128)S(1)}, u32[]{:S(2)}) copy-start(f32[12]{0:T(128)S(1)} %get-tuple-element.714) | copy-start | bytes 148
  26.2 306.5 %copy-start.49 = (f32[12]{0:T(128)}, f32[12]{0:T(128)S(1)}, u32[]{:S(2)}) copy-start(f32[12]{0:T(128)S(1)} %get-tuple-element.633) | copy-start | bytes 148
  28.3 304.5 %copy-start.7 = (f32[12,1]{0,1:T(1,128)}, f32[12,1]{0,1:T(1,128)S(1)}, u32[]{:S(2)}) copy-start(f32[12,1]{0,1:T(1,128)S(1)} %get-tuple-element.617) | copy-start | bytes 148
  28.3 304.5 %copy-start.10 = (f32[12,1]{0,1:T(1,128)}, f32[12,1]{0,1:T(1,128)S(1)}, u32[]{:S(2)}) copy-start(f32[12,1]{0,1:T(1,128)S(1)} %get-tuple-element.621) | copy-start | bytes 148
  101.1 63.8 %collective-permute-start.3 = (f32[2,12,48,1,128]{4,2,3,1,0:T(8,128)S(1)}, f32[2,12,48,1,128]{4,2,3,1,0:T(8,128)S(1)}, u32[]{:S(2)}, u32[]{:S(2)}) collective-permute-start(f32[2,12,48,1,128]{4,2,3,1,0:T(8,128)S(1)} %copy.39), channel_id=1, source_target_pairs={{1,0},{2,1},{3,2},{4,3},{5,4},{6,5},{7,6},{8,7},{9,8},{10,9},{11,1... | collective-permute-start | bytes 1769480 | tf_op jit(solution)/shard_map/ppermute | solution.py:18
  105.5 59.7 %collective-permute-start.2 = (f32[2,12,48,1,128]{4,2,3,1,0:T(8,128)S(1)}, f32[2,12,48,1,128]{4,2,3,1,0:T(8,128)S(1)}, u32[]{:S(2)}, u32[]{:S(2)}) collective-permute-start(f32[2,12,48,1,128]{4,2,3,1,0:T(8,128)S(1)} %copy.39), channel_id=1, source_target_pairs={{0,1},{1,2},{2,3},{3,4},{4,5},{5,6},{6,7},{7,8},{8,9},{9,10},{10,1... | collective-permute-start | bytes 1769480 | tf_op jit(solution)/shard_map/ppermute | solution.py:15
  188.1 100.3 %collective-permute-start.5 = (f32[2,12,48,1,128]{4,2,3,1,0:T(8,128)S(1)}, f32[2,12,48,1,128]{4,2,3,1,0:T(8,128)S(1)}, u32[]{:S(2)}, u32[]{:S(2)}) collective-permute-start(f32[2,12,48,1,128]{4,2,3,1,0:T(8,128)S(1)} %copy.46), channel_id=1, source_target_pairs={{1,0},{2,1},{3,2},{4,3},{5,4},{6,5},{7,6},{8,7},{9,8},{10,9},{11,1... | collective-permute-start | bytes 1769480 | tf_op jit(solution)/shard_map/ppermute | solution.py:18
  192.1 96.5 %collective-permute-start.4 = (f32[2,12,48,1,128]{4,2,3,1,0:T(8,128)S(1)}, f32[2,12,48,1,128]{4,2,3,1,0:T(8,128)S(1)}, u32[]{:S(2)}, u32[]{:S(2)}) collective-permute-start(f32[2,12,48,1,128]{4,2,3,1,0:T(8,128)S(1)} %copy.46), channel_id=1, source_target_pairs={{0,1},{1,2},{2,3},{3,4},{4,5},{5,6},{6,7},{7,8},{8,9},{9,10},{10,1... | collective-permute-start | bytes 1769480 | tf_op jit(solution)/shard_map/ppermute | solution.py:15
  339.7 227.3 %collective-permute-start.7 = (f32[2,12,48,1,128]{4,2,3,1,0:T(8,128)S(1)}, f32[2,12,48,1,128]{4,2,3,1,0:T(8,128)S(1)}, u32[]{:S(2)}, u32[]{:S(2)}) collective-permute-start(f32[2,12,48,1,128]{4,2,3,1,0:T(8,128)S(1)} %copy.53), channel_id=1, source_target_pairs={{1,0},{2,1},{3,2},{4,3},{5,4},{6,5},{7,6},{8,7},{9,8},{10,9},{11,1... | collective-permute-start | bytes 1769480 | tf_op jit(solution)/shard_map/ppermute | solution.py:18
  343.9 223.3 %collective-permute-start.6 = (f32[2,12,48,1,128]{4,2,3,1,0:T(8,128)S(1)}, f32[2,12,48,1,128]{4,2,3,1,0:T(8,128)S(1)}, u32[]{:S(2)}, u32[]{:S(2)}) collective-permute-start(f32[2,12,48,1,128]{4,2,3,1,0:T(8,128)S(1)} %copy.53), channel_id=1, source_target_pairs={{0,1},{1,2},{2,3},{3,4},{4,5},{5,6},{6,7},{7,8},{8,9},{9,10},{10,1... | collective-permute-start | bytes 1769480 | tf_op jit(solution)/shard_map/ppermute | solution.py:15
  618.4 248.9 %collective-permute-start.9 = (f32[2,12,48,1,128]{4,2,3,1,0:T(8,128)S(1)}, f32[2,12,48,1,128]{4,2,3,1,0:T(8,128)S(1)}, u32[]{:S(2)}, u32[]{:S(2)}) collective-permute-start(f32[2,12,48,1,128]{4,2,3,1,0:T(8,128)S(1)} %copy.60), channel_id=1, source_target_pairs={{1,0},{2,1},{3,2},{4,3},{5,4},{6,5},{7,6},{8,7},{9,8},{10,9},{11,1... | collective-permute-start | bytes 1769480 | tf_op jit(solution)/shard_map/ppermute | solution.py:18
  621.7 245.9 %collective-permute-start.8 = (f32[2,12,48,1,128]{4,2,3,1,0:T(8,128)S(1)}, f32[2,12,48,1,128]{4,2,3,1,0:T(8,128)S(1)}, u32[]{:S(2)}, u32[]{:S(2)}) collective-permute-start(f32[2,12,48,1,128]{4,2,3,1,0:T(8,128)S(1)} %copy.60), channel_id=1, source_target_pairs={{0,1},{1,2},{2,3},{3,4},{4,5},{5,6},{6,7},{7,8},{8,9},{9,10},{10,1... | collective-permute-start | bytes 1769480 | tf_op jit(solution)/shard_map/ppermute | solution.py:15
  918.8 248.3 %collective-permute-start.11 = (f32[2,12,48,1,128]{4,2,3,1,0:T(8,128)S(1)}, f32[2,12,48,1,128]{4,2,3,1,0:T(8,128)S(1)}, u32[]{:S(2)}, u32[]{:S(2)}) collective-permute-start(f32[2,12,48,1,128]{4,2,3,1,0:T(8,128)S(1)} %copy.67), channel_id=1, source_target_pairs={{1,0},{2,1},{3,2},{4,3},{5,4},{6,5},{7,6},{8,7},{9,8},{10,9},{11,1... | collective-permute-start | bytes 1769480 | tf_op jit(solution)/shard_map/ppermute | solution.py:18
  922.6 244.8 %collective-permute-start.10 = (f32[2,12,48,1,128]{4,2,3,1,0:T(8,128)S(1)}, f32[2,12,48,1,128]{4,2,3,1,0:T(8,128)S(1)}, u32[]{:S(2)}, u32[]{:S(2)}) collective-permute-start(f32[2,12,48,1,128]{4,2,3,1,0:T(8,128)S(1)} %copy.67), channel_id=1, source_target_pairs={{0,1},{1,2},{2,3},{3,4},{4,5},{5,6},{6,7},{7,8},{8,9},{9,10},{10,1... | collective-permute-start | bytes 1769480 | tf_op jit(solution)/shard_map/ppermute | solution.py:15
  (149 other events, 9407.3 us)
